TPU v7x, 32 devices: a whole 2x2x4 slice. The times are simulated.
32 devices in a mesh: island: 8 (over y, x, core), fsdp: 4 (over z).
Axes of the slice: x: 2, y: 2, z: 4, core: 2. Of those that a mesh axis runs over, the one named last changes fastest.
Arguments:
- tokens: bfloat16 [8, 1024, 8192], P('island', 'fsdp'), may hold values from -6 to 6
- cotangent: bfloat16 [8, 1024, 1024], P('island', 'fsdp'), may hold values from -0.1875 to 0.1875
- params: float32 [8, 8192, 1024], P('island', 'fsdp'), may hold values from -0.18 to 0.18
- first_moment: bfloat16 [8, 8192, 1024], P('island', 'fsdp'), may hold values from -3 to 3
- second_moment: bfloat16 [8, 8192, 1024], P('island', 'fsdp'), may hold values from 0.25 to 4
- base: float32 [8192, 512], P(('fsdp', 'island')), may hold values from -0.18 to 0.18
- outer_momentum: float32 [8192, 512], P(('fsdp', 'island')), may hold values from -0.06 to 0.06
- head_order: int32 [8], replicated, may hold values from 0 to 7, each once
- step_fragment: int32 [1], replicated, may hold values from 0 to 1
Outputs:
- params_out: float32 [8, 8192, 1024], P('island', 'fsdp')
- first_out: bfloat16 [8, 8192, 1024], P('island', 'fsdp')
- second_out: bfloat16 [8, 8192, 1024], P('island', 'fsdp')
- base_out: float32 [8192, 512], P(('fsdp', 'island'))
- momentum_out: float32 [8192, 512], P(('fsdp', 'island'))
All inputs are finite; a program needn't handle non-finite values.
Results may differ from a plain program's by a relative error of at most 0.012.
Values may be sent and summed in bfloat16 or wider, within the bound.
No kernel may reach another device: no remote copies, remote signals or barrier semaphores. Data moves between devices by JAX's collectives and lax.ppermute only.
A program may use at most 128 MiB of HBM per device.

v0:
```python
import jax
import jax.numpy as jnp
from jax import lax
from jax.sharding import PartitionSpec as P

KVH = 8
HD = 128
SYNC = 4


def outer_update(base, outer_momentum, total, islands):
    delta = base - total / islands
    momentum = 0.9 * outer_momentum + delta
    return (base - 0.7 * (delta + 0.9 * momentum), momentum)


def shards(
    tokens,
    cotangent,
    params,
    first_moment,
    second_moment,
    base,
    outer_momentum,
    head_order,
    step_fragment,
):
    local_tokens = tokens[0]
    weights = params[0]
    rows = weights.shape[0]
    width = weights.shape[1]
    block = local_tokens.shape[0]
    columns = lax.all_to_all(tokens, "fsdp", split_axis=2, concat_axis=1, tiled=True)[0]
    piece = lax.all_gather(cotangent, "fsdp", axis=1, tiled=True)
    blocks = piece.shape[1] // block

    def one_block(index, running):
        grads_part = lax.dynamic_slice_in_dim(piece[0], index * block, block, 0)
        token_part = lax.dynamic_slice_in_dim(columns, index * block, block, 0)
        part = lax.dot_general(
            token_part, grads_part, (((0,), (0,)), ((), ())), preferred_element_type=jnp.float32
        )
        part = lax.optimization_barrier(part.astype(jnp.bfloat16)).astype(jnp.float32)
        return running + part

    grad = lax.fori_loop(0, blocks, one_block, jnp.zeros((rows, width), jnp.float32))
    moment_one = 0.9 * first_moment[0].astype(jnp.float32) + 0.1 * grad
    moment_two = 0.95 * second_moment[0].astype(jnp.float32) + 0.05 * grad * grad
    stepped = weights - 0.01 * (moment_one / (jnp.sqrt(moment_two) + 1e-08) + 0.1 * weights)
    heads = lax.dynamic_slice(head_order, (step_fragment[0] * SYNC,), (SYNC,))
    shaped = stepped.reshape(rows, KVH, HD)
    fragment = jnp.take(shaped, heads, axis=1).reshape(rows, SYNC * HD)
    islands = lax.axis_size("island")
    total = lax.psum_scatter(
        fragment.astype(jnp.bfloat16), "island", scatter_dimension=0, tiled=True
    ).astype(jnp.float32)
    base_next, momentum_next = outer_update(base, outer_momentum, total, islands)
    whole_base = lax.all_gather(
        base_next.astype(jnp.bfloat16), "island", axis=0, tiled=True
    ).astype(base_next.dtype)
    updated = shaped.at[:, heads, :].set(whole_base.reshape(rows, SYNC, HD)).reshape(rows, width)
    return (
        updated[None],
        moment_one.astype(jnp.bfloat16)[None],
        moment_two.astype(jnp.bfloat16)[None],
        base_next,
        momentum_next,
    )


def solution(mesh):
    placed = (
        P("island", "fsdp", None),
        P("island", "fsdp", None),
        P("island", "fsdp", None),
        P("island", "fsdp", None),
        P("island", "fsdp", None),
        P(("fsdp", "island"), None),
        P(("fsdp", "island"), None),
        P(),
        P(),
    )
    return jax.shard_map(
        shards,
        mesh=mesh,
        in_specs=placed,
        out_specs=(
            P("island", "fsdp", None),
            P("island", "fsdp", None),
            P("island", "fsdp", None),
            P(("fsdp", "island"), None),
            P(("fsdp", "island"), None),
        ),
        check_vma=False,
    )
```

profile of v0, /device:TPU:0, one launch (start us, length us, event | category | flops | bytes accessed | tf_op | source)
XLA Modules:
  0.0 422.3 jit_solution(16253507385062909303)
XLA Ops:
  7.2 17.8 %copy.73 = bf16[1,256,8192]{1,0,2:T(2,128)(2,1)} copy(bf16[1,256,8192]{2,1,0:T(8,128)(2,1)} %param.11) | data formatting | bytes 8388608 | tf_op args[0]
  25.4 43.5 %reduce = bf16[8192,256]{1,0:T(8,128)(2,1)} reduce(bf16[8192,1,256]{2,1,0:T(2,128)(2,1)} %bitcast.56, bf16[]{:T(256)} %broadcast.57), dimensions={1}, to_apply=%bitcast.50.reduce_sub_computation | reduce | bytes 8388610
  69.0 5.1 %reshape.62 = bf16[4,2,262144]{2,1,0:T(2,128)(2,1)} reshape(bf16[8192,256]{1,0:T(8,128)(2,1)} %reduce) | data formatting | bytes 8388608
  74.1 6.3 %all-to-all-start = ((bf16[4,2,262144]{2,1,0:T(2,128)(2,1)}), bf16[4,2,262144]{2,1,0:T(2,128)(2,1)}, u32[]{:S(2)}, u32[]{:S(2)}) async-start(bf16[4,2,262144]{2,1,0:T(2,128)(2,1)} %reshape.62), calls=%async_computation | async-start | bytes 8388608 | tf_op jit(solution)/shard_map/all_to_all | solution.py:33
  82.0 9.3 %copy.71 = f32[1,2048,1024]{1,2,0:T(8,128)} copy(f32[1,2048,1024]{2,1,0:T(8,128)} %param.13) | data formatting | bytes 16777216 | tf_op args[2]
  91.3 6.6 %copy.72 = bf16[1,2048,1024]{1,2,0:T(8,128)(2,1)} copy(bf16[1,2048,1024]{2,1,0:T(8,128)(2,1)} %param.14) | data formatting | bytes 8388608 | tf_op args[3]
  97.9 6.5 %copy.76 = bf16[1,2048,1024]{1,2,0:T(8,128)(2,1)} copy(bf16[1,2048,1024]{2,1,0:T(8,128)(2,1)} %param.15) | data formatting | bytes 8388608 | tf_op args[4]
  104.6 103.0 %all-to-all-done = bf16[4,2,262144]{2,1,0:T(2,128)(2,1)} async-done(((bf16[4,2,262144]{2,1,0:T(2,128)(2,1)}), bf16[4,2,262144]{2,1,0:T(2,128)(2,1)}, u32[]{:S(2)}, u32[]{:S(2)}) %all-to-all-start) | async-done | bytes 4194336 | tf_op jit(solution)/shard_map/all_to_all | solution.py:33
  207.6 7.4 %reshape.63 = bf16[8192,1,256]{2,1,0:T(2,128)(2,1)} reshape(bf16[4,2,262144]{2,1,0:T(2,128)(2,1)} %all-to-all-done) | data formatting | bytes 8388608
  215.0 6.1 %copy.90 = bf16[1,256,8192]{1,2,0:T(8,128)(2,1)} copy(bf16[1,256,8192]{1,0,2:T(2,128)(2,1)} %bitcast.57) | data formatting | bytes 8388608
  221.1 6.2 %copy.74 = bf16[1,4,256,2048]{3,2,1,0:T(8,128)(2,1)} copy(bf16[1,4,256,2048]{2,3,1,0:T(8,128)(2,1)} %bitcast.60) | data formatting | bytes 8388608 | tf_op jit(solution)/shard_map/all_to_all | solution.py:33
  227.3 57.0 %while.14 = (s32[]{:T(128)}, f32[2048,1024]{1,0:T(8,128)}, bf16[1024,2048]{1,0:T(8,128)(2,1)}, bf16[1,1024,1024]{2,1,0:T(8,128)(2,1)}, s32[]{:T(128)}, /*index=5*/s32[]{:T(128)}, s32[]{:T(128)}, s32[]{:T(128)}) while((s32[]{:T(128)}, f32[2048,1024]{1,0:T(8,128)}, bf16[1024,2048]{1,0:T(8,128)(2,1)}, ...), condition=%wide.region_1.0_spmd.clone, body=%wide.region_0.0_spmd.clone.sunk | while | flops 1082130432 | bytes 26739852 | solution.py:46
  227.3 4.7 %convolution_convert_fusion.2 = bf16[2048,1024]{1,0:T(8,128)(2,1)} fusion(bf16[1024,2048]{1,0:T(8,128)(2,1)} %get-tuple-element.179, s32[]{:T(128)S(6)} %select_n.32, bf16[1,1024,1024]{2,1,0:T(8,128)(2,1)} %get-tuple-element.180), kind=kOutput, calls=%fused_computation.3.clone.1 | convolution fusion | flops 1075838976 | bytes 5768192 | tf_op jit(solution)/shard_map/while/body/eval_jaxpr/dot_general | solution.py:40
  231.9 7.8 %select_add_fusion.2 = f32[2048,1024]{1,0:T(8,128)} fusion(f32[2048,1024]{1,0:T(8,128)} %get-tuple-element.170, bf16[2048,1024]{1,0:T(8,128)(2,1)} %convolution_convert_fusion.2, pred[]{:T(512)S(6)} %compare.3), kind=kLoop, calls=%fused_computation.2.clone.1 | loop fusion | flops 6291456 | bytes 20971520 | tf_op jit(solution)/shard_map/while/body/eval_jaxpr/add | solution.py:44
  239.7 4.7 %convolution_convert_fusion.2 = bf16[2048,1024]{1,0:T(8,128)(2,1)} fusion(bf16[1024,2048]{1,0:T(8,128)(2,1)} %get-tuple-element.179, s32[]{:T(128)S(6)} %select_n.32, bf16[1,1024,1024]{2,1,0:T(8,128)(2,1)} %get-tuple-element.180), kind=kOutput, calls=%fused_computation.3.clone.1 | convolution fusion | flops 1075838976 | bytes 5768192 | tf_op jit(solution)/shard_map/while/body/eval_jaxpr/dot_general | solution.py:40
  244.4 10.2 %select_add_fusion.2 = f32[2048,1024]{1,0:T(8,128)} fusion(f32[2048,1024]{1,0:T(8,128)} %get-tuple-element.170, bf16[2048,1024]{1,0:T(8,128)(2,1)} %convolution_convert_fusion.2, pred[]{:T(512)S(6)} %compare.3), kind=kLoop, calls=%fused_computation.2.clone.1 | loop fusion | flops 6291456 | bytes 20971520 | tf_op jit(solution)/shard_map/while/body/eval_jaxpr/add | solution.py:44
  254.6 4.7 %convolution_convert_fusion.2 = bf16[2048,1024]{1,0:T(8,128)(2,1)} fusion(bf16[1024,2048]{1,0:T(8,128)(2,1)} %get-tuple-element.179, s32[]{:T(128)S(6)} %select_n.32, bf16[1,1024,1024]{2,1,0:T(8,128)(2,1)} %get-tuple-element.180), kind=kOutput, calls=%fused_computation.3.clone.1 | convolution fusion | flops 1075838976 | bytes 5768192 | tf_op jit(solution)/shard_map/while/body/eval_jaxpr/dot_general | solution.py:40
  259.3 10.2 %select_add_fusion.2 = f32[2048,1024]{1,0:T(8,128)} fusion(f32[2048,1024]{1,0:T(8,128)} %get-tuple-element.170, bf16[2048,1024]{1,0:T(8,128)(2,1)} %convolution_convert_fusion.2, pred[]{:T(512)S(6)} %compare.3), kind=kLoop, calls=%fused_computation.2.clone.1 | loop fusion | flops 6291456 | bytes 20971520 | tf_op jit(solution)/shard_map/while/body/eval_jaxpr/add | solution.py:44
  269.5 4.7 %convolution_convert_fusion.2 = bf16[2048,1024]{1,0:T(8,128)(2,1)} fusion(bf16[1024,2048]{1,0:T(8,128)(2,1)} %get-tuple-element.179, s32[]{:T(128)S(6)} %select_n.32, bf16[1,1024,1024]{2,1,0:T(8,128)(2,1)} %get-tuple-element.180), kind=kOutput, calls=%fused_computation.3.clone.1 | convolution fusion | flops 1075838976 | bytes 5768192 | tf_op jit(solution)/shard_map/while/body/eval_jaxpr/dot_general | solution.py:40
  274.1 10.2 %select_add_fusion.2 = f32[2048,1024]{1,0:T(8,128)} fusion(f32[2048,1024]{1,0:T(8,128)} %get-tuple-element.170, bf16[2048,1024]{1,0:T(8,128)(2,1)} %convolution_convert_fusion.2, pred[]{:T(512)S(6)} %compare.3), kind=kLoop, calls=%fused_computation.2.clone.1 | loop fusion | flops 6291456 | bytes 20971520 | tf_op jit(solution)/shard_map/while/body/eval_jaxpr/add | solution.py:44
  284.3 9.2 %copy.75 = f32[2048,1024]{0,1:T(8,128)} copy(f32[2048,1024]{1,0:T(8,128)} %get-tuple-element.84) | data formatting | bytes 16777216 | tf_op jit(solution)/shard_map/while | solution.py:46
  293.5 15.2 %fusion.9 = (bf16[1,2048,1024]{1,2,0:T(8,128)(2,1)}, f32[2048,1024]{0,1:T(8,128)}, bf16[1,2048,1024]{1,2,0:T(8,128)(2,1)}) fusion(f32[2048,1024]{0,1:T(8,128)} %copy.75, bf16[1,2048,1024]{1,2,0:T(8,128)(2,1)} %copy.76, bf16[1,2048,1024]{1,2,0:T(8,128)(2,1)} %copy.72, f32[1,2048,1024]{1,2,0:T(8,128)} %copy.71), kind=kLoop, calls=%fused_computation.17 | loop fusion | flops 35651584 | bytes 41943040 | tf_op jit(solution)/shard_map/broadcast_in_dim | solution.py:65
  308.7 4.2 gather_fusion
  315.4 39.6 %reduce-scatter.2.cloned.1.call-done = bf16[256,512]{0,1:T(8,128)(2,1)} async-done(((bf16[2048,512]{0,1:T(8,128)(2,1)}), bf16[256,512]{0,1:T(8,128)(2,1)}) %reduce-scatter.2.cloned.1.call-update) | async-done | bytes 262160 | tf_op jit(solution)/shard_map/reduce_scatter | solution.py:54
  356.9 9.2 %copy.83 = f32[2048,8,128]{2,0,1:T(8,128)} copy(f32[2048,8,128]{0,2,1:T(8,128)} %bitcast.55) | data formatting | bytes 16777216 | tf_op jit(solution)/shard_map/reshape | solution.py:51
  366.1 6.4 %copy.86 = bf16[1,2048,1024]{2,1,0:T(8,128)(2,1)} copy(bf16[1,2048,1024]{1,2,0:T(8,128)(2,1)} %get-tuple-element.134) | data formatting | bytes 8388608
  372.5 6.3 %copy.87 = bf16[1,2048,1024]{2,1,0:T(8,128)(2,1)} copy(bf16[1,2048,1024]{1,2,0:T(8,128)(2,1)} %get-tuple-element.132) | data formatting | bytes 8388608
  380.8 4.4 %all-gather.5.cloned.1.call-done = bf16[2048,512]{0,1:T(8,128)(2,1)} async-done(((bf16[256,512]{0,1:T(8,128)(2,1)}), bf16[2048,512]{0,1:T(8,128)(2,1)}) %all-gather.5.cloned.1.call-update) | async-done | bytes 2097168 | tf_op jit(solution)/shard_map/all_gather | solution.py:58
  385.2 4.1 copy.82
  389.3 8.1 %scatter_fusion = f32[2048,8,128]{2,0,1:T(8,128)} fusion(f32[2048,8,128]{2,0,1:T(8,128)} %copy.83, s32[4]{0:T(128)S(1)} %get-tuple-element.131, f32[4,2048,128]{2,1,0:T(8,128)} %bitcast.61), kind=kCustom, calls=%fused_computation.1 | custom fusion | bytes 12582928 | tf_op jit(solution)/shard_map/scatter | solution.py:61
  397.3 9.2 %copy.84 = f32[2048,8,128]{0,2,1:T(8,128)} copy(f32[2048,8,128]{2,0,1:T(8,128)} %scatter_fusion) | data formatting | bytes 16777216 | tf_op jit(solution)/shard_map/scatter | solution.py:61
  406.6 9.2 %copy.85 = f32[1,2048,1024]{2,1,0:T(8,128)} copy(f32[1,2048,1024]{1,2,0:T(8,128)} %bitcast.58) | data formatting | bytes 16777216
  (24 shorter events, 7.9 us)
Async XLA Ops:
  74.1 133.5 %all-to-all-start = ((bf16[4,2,262144]{2,1,0:T(2,128)(2,1)}), bf16[4,2,262144]{2,1,0:T(2,128)(2,1)}, u32[]{:S(2)}, u32[]{:S(2)}) async-start(bf16[4,2,262144]{2,1,0:T(2,128)(2,1)} %reshape.62), calls=%async_computation | async-start | bytes 8388608 | tf_op jit(solution)/shard_map/all_to_all | solution.py:33
  80.4 146.9 %all-gather.3.cloned.1.call-start = ((), (), s32[]{:S(2)}) async-start(), calls=%async_computation.2 | async-start | bytes 2621440 | tf_op jit(solution)/shard_map/all_gather | solution.py:34
  81.1 273.9 %reduce-scatter.2.cloned.1.call-start = ((), (), s32[]{:S(2)}) async-start(), calls=%async_computation.3 | async-start | bytes 2359296 | tf_op jit(solution)/shard_map/reduce_scatter | solution.py:54
  91.3 13.1 %copy-start.2 = (s32[8]{0:T(128)S(1)}, s32[8]{0:T(128)}, u32[]{:S(2)}) copy-start(s32[8]{0:T(128)} %param.18) | copy-start | bytes 100
  308.7 6.3 %copy-start = (f32[256,512]{1,0:T(8,128)S(1)}, f32[256,512]{1,0:T(8,128)}, u32[]{:S(2)}) copy-start(f32[256,512]{1,0:T(8,128)} %param.17) | copy-start | bytes 1572868
  308.7 6.5 %copy-start.1 = (f32[256,512]{1,0:T(8,128)S(1)}, f32[256,512]{1,0:T(8,128)}, u32[]{:S(2)}) copy-start(f32[256,512]{1,0:T(8,128)} %param.16) | copy-start | bytes 1572868
  314.7 70.4 %all-gather.5.cloned.1.call-start = ((), (), s32[]{:S(2)}) async-start(), calls=%async_computation.4 | async-start | bytes 2359296 | tf_op jit(solution)/shard_map/all_gather | solution.py:58
Sparse Core Ops, SparseCore 0:
  82.8 77.2 all-gather.2
  314.9 40.1 reduce-scatter.1
  357.1 28.0 all-gather.4
where the time goes:
time: 425 us; the launch traced here: 422 us
  waiting for transfers between devices  148 us (35%)
  local copies, waits for them, and re-layouts  134 us (32%)
  other arithmetic  101 us (24%)
  matrix products  18.6 us (4%)
  between operations  14.5 us (3%)
  starting transfers between devices  6.83 us (2%)
    all_to_all x1, waiting for transfers between devices, shards(): lax.all_to_all(tokens, 'fsdp', split_axis=2, concat_axis=1, tiled=True)[0]  103 us
    unnamed x21, local copies, waits for them, and re-layouts  83.5 us
    unnamed x2, other arithmetic  43.5 us
    reduce_scatter x1, waiting for transfers between devices, shards(): lax.psum_scatter(fragment.astype(jnp.bfloat16), 'island', scatter_dimensi...  39.6 us
    add x4, other arithmetic, one_block(): return running + part  38.4 us
    dot_general x4, matrix products, one_block(): lax.dot_general(token_part, grads_part, (((0,), (0,)), ((), ())), preferr...  18.6 us
    scatter x2, local copies, waits for them, and re-layouts, shards(): shaped.at[:, heads, :].set(whole_base.reshape(rows, SYNC, HD))  17.3 us
    broadcast_in_dim x1, other arithmetic, shards(): moment_two.astype(jnp.bfloat16)[None]  15.2 us
  transfers between devices with their start and end apart: 4, of which 3 were waited for; matrix products, arithmetic and copies ran while one was open for 16% of the time, Pallas kernels for 0%

commit v1 on v0

--- a/solution.py
+++ b/solution.py
@@ -6,6 +6,40 @@
 KVH = 8
 HD = 128
 SYNC = 4
+
+
+def point_ends(mine, dim_at, sample):
+    upper = mine.shape
+    wide_out = mine.reshape(*upper[:dim_at], sample, upper[dim_at] // sample, *upper[dim_at + 1 :])
+    row_out = jnp.moveaxis(wide_out, dim_at, 0)
+    return row_out
+
+
+def sheets_step_on(arr_in, row_dim):
+    then = list(arr_in.shape[1:])
+    then[row_dim] *= arr_in.shape[0]
+    built = jnp.moveaxis(arr_in, 0, row_dim).reshape(then)
+    return built
+
+
+def render_tables(local_x, device_axis, state, piece_in):
+    carry_out = lax.axis_size(device_axis)
+    r2 = lax.axis_index(device_axis)
+    everything, val = (carry_out, r2)
+    a_now = point_ends(local_x, state, everything)
+    steps_seen = [a_now[val]]
+    pp = 1
+    while pp < everything:
+        v1 = a_now[(val + pp) % everything]
+        steps_seen.append(
+            lax.ppermute(
+                v1, device_axis, [(dev_j, (dev_j + pp) % everything) for dev_j in range(everything)]
+            )
+        )
+        pp += 1
+    a_now = jnp.stack(steps_seen)[(val - jnp.arange(everything)) % everything]
+    t1 = sheets_step_on(a_now, piece_in)
+    return t1
 
 
 def outer_update(base, outer_momentum, total, islands):
@@ -30,7 +64,7 @@
     rows = weights.shape[0]
     width = weights.shape[1]
     block = local_tokens.shape[0]
-    columns = lax.all_to_all(tokens, "fsdp", split_axis=2, concat_axis=1, tiled=True)[0]
+    columns = render_tables(tokens, "fsdp", 2, 1)[0]
     piece = lax.all_gather(cotangent, "fsdp", axis=1, tiled=True)
     blocks = piece.shape[1] // block
 

time: 425 us -> 352 us (0.83)
  other arithmetic: 101 us -> 60.9 us
  local copies, waits for them, and re-layouts: 134 us -> 110 us
  waiting for transfers between devices: 148 us -> 139 us
    all_to_all x1 -> x0, waiting for transfers between devices: 103 us -> none  [shards(): lax.all_to_all(tokens, 'fsdp', split_axis=2, concat_axis=1, tiled=True)[0]]
    ppermute x0 -> x3, waiting for transfers between devices: none -> 72.2 us  [render_tables(): lax.ppermute(v1, device_axis, [(dev_j, (dev_j + pp) % everything) for dev...]
    unnamed x2 -> x1, other arithmetic: 43.5 us -> 0.01 us
    unnamed x21 -> x17, local copies, waits for them, and re-layouts: 83.5 us -> 53 us
    reduce_scatter x1, waiting for transfers between devices: 39.6 us -> 61.7 us  [shards(): lax.psum_scatter(fragment.astype(jnp.bfloat16), 'island', scatter_dimensi...]
    another operation x0 -> x5, local copies, waits for them, and re-layouts: none -> 8.42 us
    ppermute x0 -> x3, starting transfers between devices: none -> 7.05 us  [render_tables(): lax.ppermute(v1, device_axis, [(dev_j, (dev_j + pp) % everything) for dev...]
    all_to_all x1 -> x0, starting transfers between devices: 6.35 us -> none  [shards(): lax.all_to_all(tokens, 'fsdp', split_axis=2, concat_axis=1, tiled=True)[0]]
  transfers between devices with their start and end apart: 4 -> 6, of which waited for: 3 -> 4; matrix products, arithmetic and copies ran while one was open for 16% -> 20% of each run, Pallas kernels for 0% -> 0%
where the time goes in v1:
time: 352 us; the launch traced here: 351 us
  waiting for transfers between devices  139 us (39%)
  local copies, waits for them, and re-layouts  110 us (31%)
  other arithmetic  60.9 us (17%)
  matrix products  18.6 us (5%)
  between operations  14.6 us (4%)
  starting transfers between devices  7.35 us (2%)
    ppermute x3, waiting for transfers between devices, render_tables(): lax.ppermute(v1, device_axis, [(dev_j, (dev_j + pp) % everything) for dev...  72.2 us
    reduce_scatter x1, waiting for transfers between devices, shards(): lax.psum_scatter(fragment.astype(jnp.bfloat16), 'island', scatter_dimensi...  61.7 us
    unnamed x17, local copies, waits for them, and re-layouts  53 us
    add x4, other arithmetic, one_block(): return running + part  38.4 us
    dot_general x4, matrix products, one_block(): lax.dot_general(token_part, grads_part, (((0,), (0,)), ((), ())), preferr...  18.6 us
    scatter x2, local copies, waits for them, and re-layouts, shards(): shaped.at[:, heads, :].set(whole_base.reshape(rows, SYNC, HD))  17.2 us
    broadcast_in_dim x1, other arithmetic, shards(): moment_two.astype(jnp.bfloat16)[None]  15.2 us
    reshape x1, local copies, waits for them, and re-layouts, shards(): shaped = stepped.reshape(rows, KVH, HD)  9.2 us
  transfers between devices with their start and end apart: 6, of which 4 were waited for; matrix products, arithmetic and copies ran while one was open for 20% of the time, Pallas kernels for 0%

profile of v1, /device:TPU:0, one launch (start us, length us, event | category | flops | bytes accessed | tf_op | source)
XLA Modules:
  0.0 350.7 jit_solution(18204405647031848793)
XLA Ops:
  8.0 6.4 %copy.34 = bf16[1,256,8192]{1,2,0:T(8,128)(2,1)} copy(bf16[1,256,8192]{2,1,0:T(8,128)(2,1)} %param.11) | data formatting | bytes 8388608 | tf_op args[0]
  14.4 3.4 constant_dynamic-slice_fusion.3
  20.1 3.1 collective-permute-start
  24.6 2.6 collective-permute-start.1
  29.9 9.2 %copy.32 = f32[1,2048,1024]{1,2,0:T(8,128)} copy(f32[1,2048,1024]{2,1,0:T(8,128)} %param.13) | data formatting | bytes 16777216 | tf_op args[2]
  39.1 6.5 %copy.33 = bf16[1,2048,1024]{1,2,0:T(8,128)(2,1)} copy(bf16[1,2048,1024]{2,1,0:T(8,128)(2,1)} %param.14) | data formatting | bytes 8388608 | tf_op args[3]
  45.6 6.6 %copy.40 = bf16[1,2048,1024]{1,2,0:T(8,128)(2,1)} copy(bf16[1,2048,1024]{2,1,0:T(8,128)(2,1)} %param.15) | data formatting | bytes 8388608 | tf_op args[4]
  53.0 19.0 %collective-permute-done = bf16[1,256,2048]{2,1,0:T(8,128)(2,1)} collective-permute-done((bf16[1,256,2048]{2,1,0:T(8,128)(2,1)}, bf16[1,256,2048]{2,1,0:T(8,128)(2,1)}, u32[]{:S(2)}, u32[]{:S(2)}) %collective-permute-start) | collective-permute-done | bytes 1048608 | tf_op jit(solution)/shard_map/ppermute | solution.py:35
  72.0 53.2 %collective-permute-done.1 = bf16[1,256,2048]{2,1,0:T(8,128)(2,1)} collective-permute-done((bf16[1,256,2048]{2,1,0:T(8,128)(2,1)}, bf16[1,256,2048]{2,1,0:T(8,128)(2,1)}, u32[]{:S(2)}, u32[]{:S(2)}) %collective-permute-start.1) | collective-permute-done | bytes 1048608 | tf_op jit(solution)/shard_map/ppermute | solution.py:35
  125.2 3.6 %maximum_bitcast_fusion = bf16[4,256,2048]{2,1,0:T(8,128)(2,1)} fusion(bf16[1,1,256,2048]{3,2,1,0:T(8,128)(2,1)} %bitcast.9, bf16[1,1,256,2048]{3,2,1,0:T(8,128)(2,1)} %bitcast.7, bf16[1,1,256,2048]{3,2,1,0:T(8,128)(2,1)} %bitcast.5, bf16[1,1,256,2048]{3,2,1,0:T(8,128)(2,1)S(1)} %bitcast.67), kind=kLoop, calls=%fused_computation.20 | loop fusion | flops 6291456 | bytes 8388608 | tf_op jit(solution)/shard_map/stack | solution.py:40
  128.8 5.0 %gather_fusion = bf16[4,256,2048]{2,1,0:T(8,128)(2,1)} fusion(bf16[4,256,2048]{2,1,0:T(8,128)(2,1)} %maximum_bitcast_fusion, s32[1024]{0:T(1024)S(1)} %pad_clamp_fusion.1), kind=kCustom, calls=%fused_computation | custom fusion | bytes 8388624 | tf_op jit(solution)/shard_map/gather | solution.py:40
  133.8 57.0 %while.14 = (s32[]{:T(128)}, f32[2048,1024]{1,0:T(8,128)}, bf16[1024,2048]{1,0:T(8,128)(2,1)}, bf16[1,1024,1024]{2,1,0:T(8,128)(2,1)}, s32[]{:T(128)}, /*index=5*/s32[]{:T(128)}, s32[]{:T(128)}, s32[]{:T(128)}) while((s32[]{:T(128)}, f32[2048,1024]{1,0:T(8,128)}, bf16[1024,2048]{1,0:T(8,128)(2,1)}, ...), condition=%wide.region_1.2_spmd.clone, body=%wide.region_0.1_spmd.clone.sunk | while | flops 1082130432 | bytes 26739852 | solution.py:80
  133.8 4.7 %convolution_convert_fusion.2 = bf16[2048,1024]{1,0:T(8,128)(2,1)} fusion(bf16[1024,2048]{1,0:T(8,128)(2,1)} %get-tuple-element.173, s32[]{:T(128)S(6)} %select_n.99, bf16[1,1024,1024]{2,1,0:T(8,128)(2,1)} %get-tuple-element.174), kind=kOutput, calls=%fused_computation.4.clone.1 | convolution fusion | flops 1075838976 | bytes 5768192 | tf_op jit(solution)/shard_map/while/body/eval_jaxpr/dot_general | solution.py:74
  138.5 7.8 %select_add_fusion.2 = f32[2048,1024]{1,0:T(8,128)} fusion(f32[2048,1024]{1,0:T(8,128)} %get-tuple-element.164, bf16[2048,1024]{1,0:T(8,128)(2,1)} %convolution_convert_fusion.2, pred[]{:T(512)S(6)} %compare.13), kind=kLoop, calls=%fused_computation.3.clone.1 | loop fusion | flops 6291456 | bytes 20971520 | tf_op jit(solution)/shard_map/while/body/eval_jaxpr/add | solution.py:78
  146.3 4.7 %convolution_convert_fusion.2 = bf16[2048,1024]{1,0:T(8,128)(2,1)} fusion(bf16[1024,2048]{1,0:T(8,128)(2,1)} %get-tuple-element.173, s32[]{:T(128)S(6)} %select_n.99, bf16[1,1024,1024]{2,1,0:T(8,128)(2,1)} %get-tuple-element.174), kind=kOutput, calls=%fused_computation.4.clone.1 | convolution fusion | flops 1075838976 | bytes 5768192 | tf_op jit(solution)/shard_map/while/body/eval_jaxpr/dot_general | solution.py:74
  151.0 10.2 %select_add_fusion.2 = f32[2048,1024]{1,0:T(8,128)} fusion(f32[2048,1024]{1,0:T(8,128)} %get-tuple-element.164, bf16[2048,1024]{1,0:T(8,128)(2,1)} %convolution_convert_fusion.2, pred[]{:T(512)S(6)} %compare.13), kind=kLoop, calls=%fused_computation.3.clone.1 | loop fusion | flops 6291456 | bytes 20971520 | tf_op jit(solution)/shard_map/while/body/eval_jaxpr/add | solution.py:78
  161.2 4.7 %convolution_convert_fusion.2 = bf16[2048,1024]{1,0:T(8,128)(2,1)} fusion(bf16[1024,2048]{1,0:T(8,128)(2,1)} %get-tuple-element.173, s32[]{:T(128)S(6)} %select_n.99, bf16[1,1024,1024]{2,1,0:T(8,128)(2,1)} %get-tuple-element.174), kind=kOutput, calls=%fused_computation.4.clone.1 | convolution fusion | flops 1075838976 | bytes 5768192 | tf_op jit(solution)/shard_map/while/body/eval_jaxpr/dot_general | solution.py:74
  165.8 10.2 %select_add_fusion.2 = f32[2048,1024]{1,0:T(8,128)} fusion(f32[2048,1024]{1,0:T(8,128)} %get-tuple-element.164, bf16[2048,1024]{1,0:T(8,128)(2,1)} %convolution_convert_fusion.2, pred[]{:T(512)S(6)} %compare.13), kind=kLoop, calls=%fused_computation.3.clone.1 | loop fusion | flops 6291456 | bytes 20971520 | tf_op jit(solution)/shard_map/while/body/eval_jaxpr/add | solution.py:78
  176.0 4.7 %convolution_convert_fusion.2 = bf16[2048,1024]{1,0:T(8,128)(2,1)} fusion(bf16[1024,2048]{1,0:T(8,128)(2,1)} %get-tuple-element.173, s32[]{:T(128)S(6)} %select_n.99, bf16[1,1024,1024]{2,1,0:T(8,128)(2,1)} %get-tuple-element.174), kind=kOutput, calls=%fused_computation.4.clone.1 | convolution fusion | flops 1075838976 | bytes 5768192 | tf_op jit(solution)/shard_map/while/body/eval_jaxpr/dot_general | solution.py:74
  180.7 10.2 %select_add_fusion.2 = f32[2048,1024]{1,0:T(8,128)} fusion(f32[2048,1024]{1,0:T(8,128)} %get-tuple-element.164, bf16[2048,1024]{1,0:T(8,128)(2,1)} %convolution_convert_fusion.2, pred[]{:T(512)S(6)} %compare.13), kind=kLoop, calls=%fused_computation.3.clone.1 | loop fusion | flops 6291456 | bytes 20971520 | tf_op jit(solution)/shard_map/while/body/eval_jaxpr/add | solution.py:78
  190.9 9.1 %copy.39 = f32[2048,1024]{0,1:T(8,128)} copy(f32[2048,1024]{1,0:T(8,128)} %get-tuple-element.84) | data formatting | bytes 16777216 | tf_op jit(solution)/shard_map/while | solution.py:80
  200.0 15.2 %fusion.9 = (bf16[1,2048,1024]{1,2,0:T(8,128)(2,1)}, f32[2048,1024]{0,1:T(8,128)}, bf16[1,2048,1024]{1,2,0:T(8,128)(2,1)}) fusion(f32[2048,1024]{0,1:T(8,128)} %copy.39, bf16[1,2048,1024]{1,2,0:T(8,128)(2,1)} %copy.40, bf16[1,2048,1024]{1,2,0:T(8,128)(2,1)} %copy.33, f32[1,2048,1024]{1,2,0:T(8,128)} %copy.32), kind=kLoop, calls=%fused_computation.18 | loop fusion | flops 35651584 | bytes 41943040 | tf_op jit(solution)/shard_map/broadcast_in_dim | solution.py:99
  215.2 4.1 %gather_fusion.1 = bf16[4,2048,128]{1,2,0:T(8,128)(2,1)S(1)} fusion(f32[2048,8,128]{0,2,1:T(8,128)} %bitcast.61, s32[1024]{0:T(1024)S(1)} %pad_clamp_fusion), kind=kCustom, calls=%fused_computation.1 | custom fusion | bytes 4194320 | tf_op jit(solution)/shard_map/jit(_take)/gather | solution.py:86
  221.8 61.7 %reduce-scatter.2.cloned.1.call-done = bf16[256,512]{0,1:T(8,128)(2,1)} async-done(((bf16[2048,512]{0,1:T(8,128)(2,1)}), bf16[256,512]{0,1:T(8,128)(2,1)}) %reduce-scatter.2.cloned.1.call-update) | async-done | bytes 262160 | tf_op jit(solution)/shard_map/reduce_scatter | solution.py:88
  285.4 9.2 %copy.47 = f32[2048,8,128]{2,0,1:T(8,128)} copy(f32[2048,8,128]{0,2,1:T(8,128)} %bitcast.62) | data formatting | bytes 16777216 | tf_op jit(solution)/shard_map/reshape | solution.py:85
  294.6 6.4 %copy.50 = bf16[1,2048,1024]{2,1,0:T(8,128)(2,1)} copy(bf16[1,2048,1024]{1,2,0:T(8,128)(2,1)} %get-tuple-element.124) | data formatting | bytes 8388608
  301.0 6.3 %copy.51 = bf16[1,2048,1024]{2,1,0:T(8,128)(2,1)} copy(bf16[1,2048,1024]{1,2,0:T(8,128)(2,1)} %get-tuple-element.122) | data formatting | bytes 8388608
  309.2 4.4 %all-gather.5.cloned.1.call-done = bf16[2048,512]{0,1:T(8,128)(2,1)} async-done(((bf16[256,512]{0,1:T(8,128)(2,1)}), bf16[2048,512]{0,1:T(8,128)(2,1)}) %all-gather.5.cloned.1.call-update) | async-done | bytes 2097168 | tf_op jit(solution)/shard_map/all_gather | solution.py:92
  313.6 4.1 %copy.46 = f32[2048,4,128]{2,0,1:T(8,128)} copy(bf16[2048,4,128]{0,2,1:T(8,128)(2,1)} %bitcast.68) | data formatting | bytes 6291456 | tf_op jit(solution)/shard_map/reshape | solution.py:95
  317.7 8.0 %scatter_fusion = f32[2048,8,128]{2,0,1:T(8,128)} fusion(f32[2048,8,128]{2,0,1:T(8,128)} %copy.47, s32[4]{0:T(128)S(1)} %get-tuple-element.121, f32[4,2048,128]{2,1,0:T(8,128)} %bitcast.66), kind=kCustom, calls=%fused_computation.2 | custom fusion | bytes 12582928 | tf_op jit(solution)/shard_map/scatter | solution.py:95
  325.8 9.1 %copy.48 = f32[2048,8,128]{0,2,1:T(8,128)} copy(f32[2048,8,128]{2,0,1:T(8,128)} %scatter_fusion) | data formatting | bytes 16777216 | tf_op jit(solution)/shard_map/scatter | solution.py:95
  334.9 9.2 %copy.49 = f32[1,2048,1024]{2,1,0:T(8,128)} copy(f32[1,2048,1024]{1,2,0:T(8,128)} %bitcast.63) | data formatting | bytes 16777216
  (31 shorter events, 13.6 us)
Async XLA Ops:
  7.2 126.7 %all-gather.3.cloned.1.call-start = ((), (), s32[]{:S(2)}) async-start(), calls=%async_computation.1 | async-start | bytes 2621440 | tf_op jit(solution)/shard_map/all_gather | solution.py:68
  7.9 275.6 %reduce-scatter.2.cloned.1.call-start = ((), (), s32[]{:S(2)}) async-start(), calls=%async_computation.2 | async-start | bytes 2359296 | tf_op jit(solution)/shard_map/reduce_scatter | solution.py:88
  20.1 51.9 %collective-permute-start = (bf16[1,256,2048]{2,1,0:T(8,128)(2,1)}, bf16[1,256,2048]{2,1,0:T(8,128)(2,1)}, u32[]{:S(2)}, u32[]{:S(2)}) collective-permute-start(bf16[1,256,2048]{2,1,0:T(8,128)(2,1)} %bitcast.69), channel_id=1, source_target_pairs={{0,1},{1,2},{2,3},{3,0},{4,5},{5,6},{6,7},{7,4},{8,9},{9,10},{10,1... | collective-permute-start | bytes 3145736 | tf_op jit(solution)/shard_map/ppermute | solution.py:35
  24.6 100.6 %collective-permute-start.1 = (bf16[1,256,2048]{2,1,0:T(8,128)(2,1)}, bf16[1,256,2048]{2,1,0:T(8,128)(2,1)}, u32[]{:S(2)}, u32[]{:S(2)}) collective-permute-start(bf16[1,256,2048]{2,1,0:T(8,128)(2,1)} %bitcast.70), channel_id=1, source_target_pairs={{0,2},{1,3},{2,0},{3,1},{4,6},{5,7},{6,4},{7,5},{8,10},{9,11},{10,... | collective-permute-start | bytes 3145736 | tf_op jit(solution)/shard_map/ppermute | solution.py:35
  27.8 97.4 %collective-permute-start.2 = (bf16[1,256,2048]{2,1,0:T(8,128)(2,1)S(1)}, bf16[1,256,2048]{2,1,0:T(8,128)(2,1)}, u32[]{:S(2)}, u32[]{:S(2)}) collective-permute-start(bf16[1,256,2048]{2,1,0:T(8,128)(2,1)S(1)} %bitcast.71), channel_id=1, source_target_pairs={{0,3},{1,0},{2,1},{3,2},{4,7},{5,4},{6,5},{7,6},{8,11},{9,8},{10,9... | collective-permute-start | bytes 3145736 | tf_op jit(solution)/shard_map/ppermute | solution.py:35
  45.6 7.2 %copy-start.2 = (s32[8]{0:T(128)S(1)}, s32[8]{0:T(128)}, u32[]{:S(2)}) copy-start(s32[8]{0:T(128)} %param.18) | copy-start | bytes 100
  219.3 2.0 copy-start
  219.4 2.2 copy-start.1
  221.1 92.5 %all-gather.5.cloned.1.call-start = ((), (), s32[]{:S(2)}) async-start(), calls=%async_computation.3 | async-start | bytes 2359296 | tf_op jit(solution)/shard_map/all_gather | solution.py:92
Sparse Core Ops, SparseCore 0:
  9.5 108.5 all-gather.2
  221.3 62.2 reduce-scatter.1
  285.5 28.0 all-gather.4
